TPU v7x, 32 devices: a whole 2x2x4 slice. The times are simulated.
32 devices in a mesh: ctx: 8 (over z, x), chan: 4 (over y, core).
Axes of the slice: x: 2, y: 2, z: 4, core: 2. Of those that a mesh axis runs over, the one named last changes fastest.
Arguments:
- query_in: bfloat16 [4096, 1024], P('chan', 'ctx'), may hold values from -6 to 6
- key_in: bfloat16 [4096, 1024], P('chan', 'ctx'), may hold values from -6 to 6
- value_in: bfloat16 [4096, 1024], P('chan', 'ctx'), may hold values from -6 to 6
- short_kernel: float32 [3, 3, 4096], P(None, None, 'chan'), may hold values from -3.5 to 3.5
- filter_in: float32 [64, 64], replicated, may hold values from -0.75 to 0.75
- filter_out: float32 [64, 4096], P(None, 'chan'), may hold values from -0.75 to 0.75
- filter_decay: float32 [4096], P('chan'), may hold values from 0.5 to 40
- skip_gain: float32 [4096], P('chan'), may hold values from -3 to 3
- grad_out: bfloat16 [4096, 1024], P('chan', 'ctx'), may hold values from -6 to 6
Outputs:
- output: bfloat16 [4096, 1024], P('chan', 'ctx')
- grad_query: bfloat16 [4096, 1024], P('chan', 'ctx')
- grad_key: bfloat16 [4096, 1024], P('chan', 'ctx')
- grad_value: bfloat16 [4096, 1024], P('chan', 'ctx')
- grad_short: float32 [3, 3, 4096], P(None, None, 'chan')
- grad_filter_in: float32 [64, 64], replicated
- grad_filter_out: float32 [64, 4096], P(None, 'chan')
- grad_decay: float32 [4096], P('chan')
- grad_skip: float32 [4096], P('chan')
All inputs are finite; a program needn't handle non-finite values.
Results may differ from a plain program's by a relative error of at most 0.0006.
Values may be sent and summed in bfloat16 or wider, within the bound.
No kernel may reach another device: no remote copies, remote signals or barrier semaphores. Data moves between devices by JAX's collectives and lax.ppermute only.
A program may use at most 128 MiB of HBM per device.

v0:
```python
import math
import jax
import jax.numpy as jnp
from jax import lax
from jax.sharding import PartitionSpec as P

PRECISE = lax.Precision.HIGHEST


def shifted(value, axis, by):
    peers = lax.axis_size(axis)
    pairs = [(i, i + by) for i in range(peers) if 0 <= i + by < peers]
    return lax.ppermute(value, axis, pairs)


def position_features(position, sequence, feature_rows):
    bands = jnp.arange(feature_rows // 2, dtype=jnp.int32)
    factor = 4 * (bands + 1) * (bands + 1)
    phase = position[None, :] * factor[:, None] % sequence
    angles = 2.0 * math.pi / sequence * phase.astype(jnp.float32)
    return jnp.concatenate([jnp.cos(angles), jnp.sin(angles)], axis=0)


def angle_tables(left_index, right_index, modulus):
    phase = left_index[:, None] * right_index[None, :] % modulus
    angles = 2.0 * math.pi / modulus * phase.astype(jnp.float32)
    return (jnp.cos(angles), jnp.sin(angles))


def contract(form, left, right):
    return jnp.einsum(form, left, right, precision=PRECISE)


def times_forward(real_part, imag_part, cosine, sine):
    return (real_part * cosine + imag_part * sine, imag_part * cosine - real_part * sine)


def times_inverse(real_part, imag_part, cosine, sine):
    return (real_part * cosine - imag_part * sine, imag_part * cosine + real_part * sine)


def complex_times(first_real, first_imag, second_real, second_imag):
    return (
        first_real * second_real - first_imag * second_imag,
        first_real * second_imag + first_imag * second_real,
    )


def local_forward(real_part, imag_part):
    length = real_part.shape[-1]
    inner = 64
    outer = length // inner
    leading = real_part.shape[:-1]
    real_part = real_part.reshape(leading + (outer, inner))
    imag_part = imag_part.reshape(leading + (outer, inner))
    outer_index = jnp.arange(outer, dtype=jnp.int32)
    inner_index = jnp.arange(inner, dtype=jnp.int32)
    cos_outer, sin_outer = angle_tables(outer_index, outer_index, outer)
    first_real = contract("cb,...ba->...ca", cos_outer, real_part) + contract(
        "cb,...ba->...ca", sin_outer, imag_part
    )
    first_imag = contract("cb,...ba->...ca", cos_outer, imag_part) - contract(
        "cb,...ba->...ca", sin_outer, real_part
    )
    cos_middle, sin_middle = angle_tables(outer_index, inner_index, length)
    first_real, first_imag = times_forward(first_real, first_imag, cos_middle, sin_middle)
    cos_inner, sin_inner = angle_tables(inner_index, inner_index, inner)
    final_real = contract("...ca,da->...cd", first_real, cos_inner) + contract(
        "...ca,da->...cd", first_imag, sin_inner
    )
    final_imag = contract("...ca,da->...cd", first_imag, cos_inner) - contract(
        "...ca,da->...cd", first_real, sin_inner
    )
    return (final_real, final_imag)


def local_inverse(real_part, imag_part):
    outer = real_part.shape[-2]
    inner = real_part.shape[-1]
    length = outer * inner
    leading = real_part.shape[:-2]
    outer_index = jnp.arange(outer, dtype=jnp.int32)
    inner_index = jnp.arange(inner, dtype=jnp.int32)
    cos_inner, sin_inner = angle_tables(inner_index, inner_index, inner)
    first_real = contract("...cd,ad->...ca", real_part, cos_inner) - contract(
        "...cd,ad->...ca", imag_part, sin_inner
    )
    first_imag = contract("...cd,ad->...ca", imag_part, cos_inner) + contract(
        "...cd,ad->...ca", real_part, sin_inner
    )
    cos_middle, sin_middle = angle_tables(outer_index, inner_index, length)
    first_real, first_imag = times_inverse(first_real, first_imag, cos_middle, sin_middle)
    cos_outer, sin_outer = angle_tables(outer_index, outer_index, outer)
    final_real = contract("bc,...ca->...ba", cos_outer, first_real) - contract(
        "bc,...ca->...ba", sin_outer, first_imag
    )
    final_imag = contract("bc,...ca->...ba", cos_outer, first_imag) + contract(
        "bc,...ca->...ba", sin_outer, first_real
    )
    return (final_real.reshape(leading + (length,)), final_imag.reshape(leading + (length,)))


def held_frequencies(device):
    return 2 * device + jnp.arange(2, dtype=jnp.int32)


def forward_spectrum(signals):
    shards = lax.axis_size("ctx")
    device = lax.axis_index("ctx")
    signal_count, channels, length = signals.shape
    padded = 2 * shards * length
    columns = lax.all_to_all(
        signals.reshape((1, signal_count, channels, length)),
        "ctx",
        split_axis=3,
        concat_axis=0,
        tiled=True,
    )
    shard_index = jnp.arange(shards, dtype=jnp.int32)
    freq_index = jnp.arange(2 * shards, dtype=jnp.int32)
    cos_table, sin_table = angle_tables(freq_index, shard_index, 2 * shards)
    rows_real = contract("qp,pmgb->qmgb", cos_table, columns)
    rows_imag = -contract("qp,pmgb->qmgb", sin_table, columns)
    arrived = lax.all_to_all(
        jnp.stack([rows_real, rows_imag]), "ctx", split_axis=1, concat_axis=4, tiled=True
    )
    spec_real = arrived[0]
    spec_imag = arrived[1]
    freqs = held_frequencies(device)
    cosine, sine = angle_tables(freqs, jnp.arange(length, dtype=jnp.int32), padded)
    spec_real, spec_imag = times_forward(
        spec_real, spec_imag, cosine[:, None, None, :], sine[:, None, None, :]
    )
    return local_forward(spec_real, spec_imag)


def inverse_columns(spec_real, spec_imag):
    shards = lax.axis_size("ctx")
    device = lax.axis_index("ctx")
    real_part, imag_part = local_inverse(spec_real, spec_imag)
    length = real_part.shape[-1]
    padded = 2 * shards * length
    freqs = held_frequencies(device)
    cosine, sine = angle_tables(freqs, jnp.arange(length, dtype=jnp.int32), padded)
    real_part, imag_part = times_inverse(
        real_part, imag_part, cosine[:, None, None, :], sine[:, None, None, :]
    )
    shard_index = jnp.arange(shards, dtype=jnp.int32)
    arrived = lax.all_to_all(
        jnp.stack([real_part, imag_part]), "ctx", split_axis=4, concat_axis=1, tiled=True
    )
    cos_table, sin_table = angle_tables(
        shard_index, jnp.arange(2 * shards, dtype=jnp.int32), 2 * shards
    )
    columns = contract("pq,qmgb->pmgb", cos_table, arrived[0]) - contract(
        "pq,qmgb->pmgb", sin_table, arrived[1]
    )
    return columns * (1.0 / padded)


def to_tokens(columns):
    arrived = lax.all_to_all(columns, "ctx", split_axis=0, concat_axis=3, tiled=True)
    return arrived[0]


def body(
    query_in,
    key_in,
    value_in,
    short_kernel,
    filter_in,
    filter_out,
    filter_decay,
    skip_gain,
    grad_out,
):
    shards = lax.axis_size("ctx")
    device = lax.axis_index("ctx")
    length = query_in.shape[1]
    sequence = shards * length
    scale = sequence ** (-0.5)
    inputs = jnp.stack([query_in, key_in, value_in])
    rim = shifted(inputs[:, :, -2:], "ctx", 1)
    values = inputs.astype(jnp.float32)
    rim_values = rim.astype(jnp.float32)
    before_one = jnp.concatenate([rim_values[..., 1:], values[..., :-1]], axis=-1)
    before_two = jnp.concatenate([rim_values, values[..., :-2]], axis=-1)
    kernel = short_kernel[:, :, :, None]
    shorted = kernel[:, 0] * values + kernel[:, 1] * before_one + kernel[:, 2] * before_two
    query_short = shorted[0]
    key_short = shorted[1]
    value_short = shorted[2]
    gate = key_short * value_short
    position = device * length + jnp.arange(length, dtype=jnp.int32)
    fraction = position.astype(jnp.float32) / sequence
    basis = position_features(position, sequence, filter_in.shape[0])
    preact = jnp.dot(filter_in.T, basis, precision=PRECISE)
    hidden = jnp.sin(preact)
    window = jnp.exp(-filter_decay[:, None] * fraction[None, :])
    taps = window * jnp.dot(filter_out.T, hidden, precision=PRECISE) * scale
    spec_real, spec_imag = forward_spectrum(jnp.stack([gate, taps]))
    gate_real, gate_imag = (spec_real[:, 0], spec_imag[:, 0])
    taps_real, taps_imag = (spec_real[:, 1], spec_imag[:, 1])
    prod_real, prod_imag = complex_times(gate_real, gate_imag, taps_real, taps_imag)
    conv = to_tokens(inverse_columns(prod_real[:, None], prod_imag[:, None]))[0]
    mixed = conv + skip_gain[:, None] * gate
    output = (query_short * mixed).astype(jnp.bfloat16)
    upstream = grad_out.astype(jnp.float32)
    grad_mixed = upstream * query_short
    grad_query_short = upstream * mixed
    upper_real, upper_imag = forward_spectrum(grad_mixed[None])
    upper_real = upper_real[:, 0]
    upper_imag = upper_imag[:, 0]
    along_real, along_imag = complex_times(taps_real, -taps_imag, upper_real, upper_imag)
    cross_real, cross_imag = complex_times(gate_real, -gate_imag, upper_real, upper_imag)
    backward = to_tokens(
        inverse_columns(
            jnp.stack([along_real, cross_real], axis=1), jnp.stack([along_imag, cross_imag], axis=1)
        )
    )
    grad_gate = backward[0] + skip_gain[:, None] * grad_mixed
    grad_taps = backward[1]
    grads = jnp.stack([grad_query_short, grad_gate * value_short, grad_gate * key_short])
    after = shifted(grads[..., :2], "ctx", -1)
    next_one = jnp.concatenate([grads[..., 1:], after[..., :1]], axis=-1)
    next_two = jnp.concatenate([grads[..., 2:], after], axis=-1)
    grad_inputs = (kernel[:, 0] * grads + kernel[:, 1] * next_one + kernel[:, 2] * next_two).astype(
        jnp.bfloat16
    )
    short_terms = jnp.stack(
        [
            jnp.sum(grads * values, axis=-1),
            jnp.sum(grads * before_one, axis=-1),
            jnp.sum(grads * before_two, axis=-1),
        ],
        axis=1,
    )
    weighted = grad_taps * window * scale
    out_terms = jnp.dot(hidden, weighted.T, precision=PRECISE)
    grad_hidden = jnp.dot(filter_out, weighted, precision=PRECISE)
    in_terms = jnp.dot(basis, (grad_hidden * jnp.cos(preact)).T, precision=PRECISE)
    decay_terms = jnp.sum(grad_taps * taps * -fraction[None, :], axis=1)
    skip_terms = jnp.sum(grad_mixed * gate, axis=1)
    short_sum, out_sum, decay_sum, skip_sum = lax.psum(
        (short_terms, out_terms, decay_terms, skip_terms), "ctx"
    )
    in_sum = lax.psum(in_terms, ("ctx", "chan"))
    return (
        output,
        grad_inputs[0],
        grad_inputs[1],
        grad_inputs[2],
        short_sum * scale,
        in_sum * scale,
        out_sum * scale,
        decay_sum * scale,
        skip_sum * scale,
    )


def solution(mesh):
    placed = (
        P("chan", "ctx"),
        P("chan", "ctx"),
        P("chan", "ctx"),
        P(None, None, "chan"),
        P(),
        P(None, "chan"),
        P("chan"),
        P("chan"),
        P("chan", "ctx"),
    )
    return jax.shard_map(
        body,
        mesh=mesh,
        in_specs=placed,
        out_specs=(
            P("chan", "ctx"),
            P("chan", "ctx"),
            P("chan", "ctx"),
            P("chan", "ctx"),
            P(None, None, "chan"),
            P(),
            P(None, "chan"),
            P("chan"),
            P("chan"),
        ),
        check_vma=False,
    )
```

profile of v0, /device:TPU:0, one launch (start us, length us, event | category | flops | bytes accessed | tf_op | source)
XLA Modules:
  0.0 651.2 jit_solution(13803028707653949594)
XLA Ops:
  11.0 4.8 collective-permute-start
  20.5 6.6 %all-to-all-start.4 = ((f32[1,1,1024,128]{2,1,0,3:T(1,128)}), f32[1,1,1024,128]{2,1,0,3:T(1,128)}, u32[]{:S(2)}, u32[]{:S(2)}) async-start(f32[1,1,1024,128]{2,1,0,3:T(1,128)} %copy.246), calls=%async_computation.4 | async-start | bytes 1048576 | tf_op jit(solution)/shard_map/all_to_all | solution.py:112
  32.8 7.8 %all-to-all-done.4 = f32[1,1,1024,128]{2,1,0,3:T(1,128)} async-done(((f32[1,1,1024,128]{2,1,0,3:T(1,128)}), f32[1,1,1024,128]{2,1,0,3:T(1,128)}, u32[]{:S(2)}, u32[]{:S(2)}) %all-to-all-start.4) | async-done | bytes 524320 | tf_op jit(solution)/shard_map/all_to_all | solution.py:112
  40.6 4.2 all-to-all-start
  51.2 18.4 %all-to-all-done = f32[1,2,1024,128]{2,1,0,3:T(2,128)} async-done(((f32[1,2,1024,128]{2,1,0,3:T(2,128)}), f32[1,2,1024,128]{2,1,0,3:T(2,128)}, u32[]{:S(2)}, u32[]{:S(2)}) %all-to-all-start) | async-done | bytes 1048608 | tf_op jit(solution)/shard_map/all_to_all | solution.py:112
  69.6 4.8 all-to-all-start.5
  74.4 3.4 negate_bitcast_fusion
  77.9 3.4 convolution_bitcast_fusion
  81.9 4.4 copy.220
  86.3 35.7 %all-to-all-done.5 = f32[2,16,1,1024,16]{3,4,2,0,1:T(8,128)} async-done(((f32[2,16,1,1024,16]{3,4,2,0,1:T(8,128)}), f32[2,16,1,1024,16]{3,4,2,0,1:T(8,128)}, u32[]{:S(2)}, u32[]{:S(2)}) %all-to-all-start.5) | async-done | bytes 2097184 | tf_op jit(solution)/shard_map/all_to_all | solution.py:124
  122.0 4.7 all-to-all-start.1
  132.9 4.1 fusion.61
  136.9 4.3 fusion.35
  141.3 4.1 fusion.65
  145.3 5.7 subtract_bitcast_fusion.1
  157.5 61.7 %all-to-all-done.1 = f32[2,16,2,1024,16]{3,4,2,0,1:T(8,128)} async-done(((f32[2,16,2,1024,16]{3,4,2,0,1:T(8,128)}), f32[2,16,2,1024,16]{3,4,2,0,1:T(8,128)}, u32[]{:S(2)}, u32[]{:S(2)}) %all-to-all-start.1) | async-done | bytes 4194336 | tf_op jit(solution)/shard_map/all_to_all | solution.py:124
  224.1 7.9 %fusion.26 = f32[2,2,1024,64,2]{2,4,3,1,0:T(2,128)S(1)} fusion(f32[2,2,1024,2,64]{2,4,3,1,0:T(8,128)S(1)} %get-tuple-element.68), kind=kOutput, calls=%fused_computation.48 | convolution fusion | flops 12582968 | bytes 4194304 | tf_op jit(solution)/shard_map/cb,...ba->...ca/dot_general | solution.py:31
  232.0 8.3 %fusion.22 = f32[2,2,1024,64,2]{2,4,3,1,0:T(2,128)S(1)} fusion(f32[2,2,1024,2,64]{2,4,3,1,0:T(8,128)S(1)} %get-tuple-element.69), kind=kOutput, calls=%fused_computation.44 | convolution fusion | flops 12582968 | bytes 4194304 | tf_op jit(solution)/shard_map/cb,...ba->...ca/dot_general | solution.py:31
  240.3 8.2 %convolution_add_fusion = f32[2,2,1024,64,2]{2,4,3,1,0:T(2,128)S(1)} fusion(f32[2,2,1024,64,2]{2,4,3,1,0:T(2,128)S(1)} %fusion.26, f32[2,2,1024,2,64]{2,4,3,1,0:T(8,128)S(1)} %get-tuple-element.69), kind=kOutput, calls=%fused_computation.42 | convolution fusion | flops 13107256 | bytes 6291456 | tf_op jit(solution)/shard_map/cb,...ba->...ca/dot_general | solution.py:31
  248.6 11.2 %fusion.2 = (f32[2,2,1024,2,64]{2,3,4,1,0:T(2,128)S(1)}, f32[2,2,1024,2,64]{2,3,4,1,0:T(2,128)S(1)}) fusion(f32[2,2,1024,64,2]{2,4,3,1,0:T(2,128)S(1)} %convolution_add_fusion, f32[2,64]{0,1:T(8,128)S(1)} %copy-done.21, f32[2,64]{0,1:T(8,128)S(1)} %copy-done.23, f32[2,2,1024,64,2]{2,4,3,1,0:T(2,128)S(1)} %fusion.22, ...), kind=kOutput, calls=%fused_computation.14 | convolution fusion | flops 16252984 | bytes 10486784 | tf_op jit(solution)/shard_map/cb,...ba->...ca/dot_general | solution.py:31
  265.4 3.1 fusion.16
  268.6 3.1 fusion.19
  271.7 3.9 multiply_subtract_fusion.3
  284.9 9.6 %multiply_subtract_fusion = (f32[2,2,1024,2,64]{2,3,4,1,0:T(2,128)S(1)}, f32[2,2,1024,2,64]{2,3,4,1,0:T(2,128)S(1)}) fusion(f32[2,64]{0,1:T(8,128)S(1)} %copy-done.21, f32[2,64]{0,1:T(8,128)S(1)} %copy-done.23, f32[2,2,1024,2,64]{2,4,3,1,0:T(8,128)S(1)} %fusion.13, f32[2,2,1024,2,64]{2,4,3,1,0:T(8,128)S(1)} %fusion.15, ...), kind=kLoop, calls=%fused_computation.23 | loop fusion | flops 4194304 | bytes 12583936 | tf_op jit(solution)/shard_map/sub | solution.py:39
  294.5 7.5 %fusion.190 = f32[2,2,1024,64,2]{2,4,3,1,0:T(2,128)S(1)} fusion(f32[2,2,1024,2,64]{2,3,4,1,0:T(2,128)S(1)} %get-tuple-element.60), kind=kOutput, calls=%fused_computation.283 | convolution fusion | flops 12582968 | bytes 4194304 | tf_op jit(solution)/shard_map/bc,...ca->...ba/dot_general | solution.py:31
  302.0 7.5 %fusion.188 = f32[2,2,1024,64,2]{2,4,3,1,0:T(2,128)S(1)} fusion(f32[2,2,1024,2,64]{2,3,4,1,0:T(2,128)S(1)} %get-tuple-element.61), kind=kOutput, calls=%fused_computation.281 | convolution fusion | flops 12582968 | bytes 4194304 | tf_op jit(solution)/shard_map/bc,...ca->...ba/dot_general | solution.py:31
  309.6 8.4 %subtract_bitcast_fusion = f32[2,2,1024,2,64]{2,3,4,1,0:T(2,128)S(1)} fusion(f32[2,2,1024,64,2]{2,4,3,1,0:T(2,128)S(1)} %fusion.190, f32[2,2,1024,2,64]{2,3,4,1,0:T(2,128)S(1)} %get-tuple-element.61), kind=kOutput, calls=%fused_computation.21 | convolution fusion | flops 13107256 | bytes 6291456 | tf_op jit(solution)/shard_map/bc,...ca->...ba/dot_general | solution.py:31
  317.9 8.0 %add_bitcast_fusion = f32[2,2,1024,2,64]{2,3,4,1,0:T(2,128)S(1)} fusion(f32[2,2,1024,64,2]{2,4,3,1,0:T(2,128)S(1)} %fusion.188, f32[2,2,1024,2,64]{2,3,4,1,0:T(2,128)S(1)} %get-tuple-element.60), kind=kOutput, calls=%fused_computation.20 | convolution fusion | flops 13107256 | bytes 6291456 | tf_op jit(solution)/shard_map/bc,...ca->...ba/dot_general | solution.py:31
  328.8 5.2 copy.268
  334.0 5.0 all-to-all-start.6
  345.8 4.1 fusion.67
  349.8 4.3 fusion.37
  354.5 4.1 fusion.71
  358.5 4.4 fusion.38
  366.8 64.8 %all-to-all-done.6 = f32[2,2,2,1024,128]{3,2,1,0,4:T(2,128)} async-done(((f32[2,2,2,1024,128]{3,2,1,0,4:T(2,128)}), f32[2,2,2,1024,128]{3,2,1,0,4:T(2,128)}, u32[]{:S(2)}, u32[]{:S(2)}) %all-to-all-start.6) | async-done | bytes 4194336 | tf_op jit(solution)/shard_map/all_to_all | solution.py:149
  431.5 4.4 all-to-all-start.2
  435.9 4.6 copy.269
  445.3 3.7 squeeze.65
  449.1 4.6 copy.270
  453.7 3.7 squeeze.64
  462.9 20.8 %all-to-all-done.2 = f32[2,2,1,1024,128]{3,1,2,0,4:T(2,128)} async-done(((f32[2,2,1,1024,128]{3,1,2,0,4:T(2,128)}), f32[2,2,1,1024,128]{3,1,2,0,4:T(2,128)}, u32[]{:S(2)}, u32[]{:S(2)}) %all-to-all-start.2) | async-done | bytes 2097184 | tf_op jit(solution)/shard_map/all_to_all | solution.py:149
  483.7 4.5 all-to-all-start.7
  496.9 3.0 copy.242
  506.5 7.3 %all-to-all-done.7 = f32[8,2,1024,16]{2,3,1,0:T(8,128)} async-done(((f32[8,2,1024,16]{2,3,1,0:T(8,128)}), f32[8,2,1024,16]{2,3,1,0:T(8,128)}, u32[]{:S(2)}, u32[]{:S(2)}) %all-to-all-start.7) | async-done | bytes 1048608 | tf_op jit(solution)/shard_map/all_to_all | solution.py:162
  513.8 4.1 all-to-all-start.3
  523.4 40.9 %psum.36 = f32[64,64]{1,0:T(8,128)S(1)} all-reduce(f32[64,64]{1,0:T(8,128)} %fusion.105), channel_id=1, replica_groups=mesh['ctx'=8,'chan'=4] {'ctx','chan'}, use_global_device_ids=true, to_apply=%region_4.5 | all-reduce | flops 4096 | bytes 32768 | tf_op jit(solution)/shard_map/psum | solution.py:247
  574.1 37.3 %all-reduce = (f32[3,3,1024]{2,0,1:T(4,128)S(1)}, f32[1024]{0:T(1024)S(1)}, f32[1024]{0:T(1024)S(1)}) all-reduce(f32[3,3,1024]{2,0,1:T(4,128)S(1)} %pad_maximum_fusion.14, f32[1024]{0:T(1024)S(1)} %get-tuple-element.106, f32[1024]{0:T(1024)S(1)} %get-tuple-element.96), channel_id=1, replica_groups=mesh['ctx'=8,'chan'=4] {'ctx'}, use_global_device_ids=true, to_apply=%region_3.4 | all-reduce | flops 11264 | bytes 90112 | tf_op jit(solution)/shard_map/psum | solution.py:244
  621.0 21.3 %all-reduce.3.cloned.1.call-done = f32[64,1024]{1,0:T(8,128)} async-done(((f32[64,1024]{1,0:T(8,128)}), f32[64,1024]{1,0:T(8,128)}) %all-reduce.3.cloned.1.call-update) | async-done | bytes 262160 | tf_op jit(solution)/shard_map/psum | solution.py:244
  (188 shorter events, 118.8 us)
Async XLA Ops:
  7.2 22.2 %copy-start = (f32[64,1024]{1,0:T(8,128)S(1)}, f32[64,1024]{1,0:T(8,128)}, u32[]{:S(2)}) copy-start(f32[64,1024]{1,0:T(8,128)} %param.14) | copy-start | bytes 786436
  8.3 2.6 copy-start.10
  8.3 7.5 %copy-start.27 = (f32[3,3,1024]{2,1,0:T(4,128)S(1)}, f32[3,3,1024]{2,1,0:T(4,128)}, u32[]{:S(2)}) copy-start(f32[3,3,1024]{2,1,0:T(4,128)} %param.12) | copy-start | bytes 110596
  8.3 7.7 %copy-start.36 = (f32[1024]{0:T(1024)S(1)}, f32[1024]{0:T(1024)}, u32[]{:S(2)}) copy-start(f32[1024]{0:T(1024)} %param.15) | copy-start | bytes 12292
  8.4 7.8 %copy-start.19 = (bf16[1024,128]{1,0:T(8,128)(2,1)S(1)}, bf16[1024,128]{1,0:T(8,128)(2,1)}, u32[]{:S(2)}) copy-start(bf16[1024,128]{1,0:T(8,128)(2,1)} %param.17) | copy-start | bytes 786436
  9.6 7.4 %copy-start.11 = (bf16[1024,128]{0,1:T(8,128)(2,1)}, bf16[1024,128]{0,1:T(8,128)(2,1)S(1)}, u32[]{:S(2)}) copy-start(bf16[1024,128]{0,1:T(8,128)(2,1)S(1)} %copy.215) | copy-start | bytes 786436
  10.8 6.5 copy-start.12
  11.0 6.2 collective-permute-start
  17.3 1.8 copy-start.25
  17.3 1.7 copy-start.18
  20.5 20.0 %all-to-all-start.4 = ((f32[1,1,1024,128]{2,1,0,3:T(1,128)}), f32[1,1,1024,128]{2,1,0,3:T(1,128)}, u32[]{:S(2)}, u32[]{:S(2)}) async-start(f32[1,1,1024,128]{2,1,0,3:T(1,128)} %copy.246), calls=%async_computation.4 | async-start | bytes 1048576 | tf_op jit(solution)/shard_map/all_to_all | solution.py:112
  27.7 1.7 copy-start.37
  30.1 0.8 copy-start.8
  40.6 29.0 %all-to-all-start = ((f32[1,2,1024,128]{2,1,0,3:T(2,128)}), f32[1,2,1024,128]{2,1,0,3:T(2,128)}, u32[]{:S(2)}, u32[]{:S(2)}) async-start(f32[1,2,1024,128]{2,1,0,3:T(2,128)} %copy.217), calls=%async_computation | async-start | bytes 2097152 | tf_op jit(solution)/shard_map/all_to_all | solution.py:112
  69.6 52.4 %all-to-all-start.5 = ((f32[2,16,1,1024,16]{3,4,2,0,1:T(8,128)}), f32[2,16,1,1024,16]{3,4,2,0,1:T(8,128)}, u32[]{:S(2)}, u32[]{:S(2)}) async-start(f32[2,16,1,1024,16]{3,4,2,0,1:T(8,128)} %copy.248), calls=%async_computation.5 | async-start | bytes 4194304 | tf_op jit(solution)/shard_map/all_to_all | solution.py:124
  122.0 97.3 %all-to-all-start.1 = ((f32[2,16,2,1024,16]{3,4,2,0,1:T(8,128)}), f32[2,16,2,1024,16]{3,4,2,0,1:T(8,128)}, u32[]{:S(2)}, u32[]{:S(2)}) async-start(f32[2,16,2,1024,16]{3,4,2,0,1:T(8,128)} %copy.220), calls=%async_computation.1 | async-start | bytes 8388608 | tf_op jit(solution)/shard_map/all_to_all | solution.py:124
  127.4 2.1 copy-start.30
  130.3 2.2 copy-start.28
  141.2 4.1 copy-start.20
  141.2 4.1 copy-start.22
  151.1 4.0 copy-start.15
  222.6 0.7 copy-start.29
  240.3 8.3 %copy-start.21 = (f32[2,64]{0,1:T(8,128)S(1)}, f32[2,64]{0,1:T(8,128)}, u32[]{:S(2)}) copy-start(f32[2,64]{0,1:T(8,128)} %copy.229) | copy-start | bytes 1540
  240.3 8.3 %copy-start.23 = (f32[2,64]{0,1:T(8,128)S(1)}, f32[2,64]{0,1:T(8,128)}, u32[]{:S(2)}) copy-start(f32[2,64]{0,1:T(8,128)} %copy.226) | copy-start | bytes 1540
  268.5 3.1 copy-start.14
  268.6 3.1 copy-start.16
  268.6 3.1 copy-start.17
  326.5 0.7 copy-start.33
  334.0 97.5 %all-to-all-start.6 = ((f32[2,2,2,1024,128]{3,2,1,0,4:T(2,128)}), f32[2,2,2,1024,128]{3,2,1,0,4:T(2,128)}, u32[]{:S(2)}, u32[]{:S(2)}) async-start(f32[2,2,2,1024,128]{3,2,1,0,4:T(2,128)} %copy.268), calls=%async_computation.6 | async-start | bytes 8388608 | tf_op jit(solution)/shard_map/all_to_all | solution.py:149
  339.0 2.6 copy-start.1
  339.0 3.8 copy-start.2
  342.9 1.3 copy-start.31
  342.9 1.3 copy-start.32
  358.5 4.7 copy-start.35
  431.5 52.2 %all-to-all-start.2 = ((f32[2,2,1,1024,128]{3,1,2,0,4:T(2,128)}), f32[2,2,1,1024,128]{3,1,2,0,4:T(2,128)}, u32[]{:S(2)}, u32[]{:S(2)}) async-start(f32[2,2,1,1024,128]{3,1,2,0,4:T(2,128)} %copy.240), calls=%async_computation.2 | async-start | bytes 4194304 | tf_op jit(solution)/shard_map/all_to_all | solution.py:149
  457.3 2.9 copy-start.3
  483.7 30.1 %all-to-all-start.7 = ((f32[8,2,1024,16]{2,3,1,0:T(8,128)}), f32[8,2,1024,16]{2,3,1,0:T(8,128)}, u32[]{:S(2)}, u32[]{:S(2)}) async-start(f32[8,2,1024,16]{2,3,1,0:T(8,128)} %copy.272), calls=%async_computation.7 | async-start | bytes 2097152 | tf_op jit(solution)/shard_map/all_to_all | solution.py:162
  502.8 2.0 copy-start.13
  513.8 53.3 %all-to-all-start.3 = ((f32[8,1,1024,16]{2,3,1,0:T(8,128)}), f32[8,1,1024,16]{2,3,1,0:T(8,128)}, u32[]{:S(2)}, u32[]{:S(2)}) async-start(f32[8,1,1024,16]{2,3,1,0:T(8,128)} %copy.244), calls=%async_computation.3 | async-start | bytes 1048576 | tf_op jit(solution)/shard_map/all_to_all | solution.py:162
  517.9 124.3 %all-reduce.3.cloned.1.call-start = ((), (), s32[]{:S(2)}) async-start(), calls=%async_computation.8 | async-start | bytes 524288 | tf_op jit(solution)/shard_map/psum | solution.py:244
  518.0 2.2 copy-start.9
  518.0 3.9 copy-start.24
  521.1 0.8 copy-start.7
  567.0 4.7 copy-start.26
  612.0 5.7 collective-permute-start.1
  614.1 3.7 copy-start.4
  614.1 3.7 copy-start.5
  614.1 3.7 copy-start.6
  (1 other events, 0.7 us)
Sparse Core Ops, SparseCore 0:
  571.8 70.4 all-reduce.2
where the time goes:
time: 659 us; the launch traced here: 651 us
  waiting for transfers between devices  241 us (37%)
  matrix products  162 us (25%)
  local copies, waits for them, and re-layouts  82.3 us (12%)
  blocking collectives  78.2 us (12%)
  starting transfers between devices  44.5 us (7%)
  other arithmetic  28.1 us (4%)
  between operations  15.7 us (2%)
    dot_general x40, matrix products, contract(): return jnp.einsum(form, left, right, precision=PRECISE)  156 us
    all_to_all x2, waiting for transfers between devices, forward_spectrum(): lax.all_to_all(jnp.stack([rows_real, rows_imag]), 'ctx', split_axis=1, co...  97.4 us
    all_to_all x2, waiting for transfers between devices, inverse_columns(): lax.all_to_all(jnp.stack([real_part, imag_part]), 'ctx', split_axis=4, co...  85.6 us
    psum x1, blocking collectives, body(): in_sum = lax.psum(in_terms, ('ctx', 'chan'))  40.9 us
    psum x1, blocking collectives, body(): lax.psum((short_terms, out_terms, decay_terms, skip_terms), 'ctx')  37.3 us
    all_to_all x2, waiting for transfers between devices, forward_spectrum(): lax.all_to_all(signals.reshape((1, signal_count, channels, length)), 'ctx...  26.2 us
    psum x1, waiting for transfers between devices, body(): lax.psum((short_terms, out_terms, decay_terms, skip_terms), 'ctx')  21.3 us
  transfers between devices with their start and end apart: 11, of which 10 were waited for; matrix products, arithmetic and copies ran while one was open for 22% of the time, Pallas kernels for 0%

commit v1 on v0

--- a/solution.py
+++ b/solution.py
@@ -244,7 +244,7 @@
     short_sum, out_sum, decay_sum, skip_sum = lax.psum(
         (short_terms, out_terms, decay_terms, skip_terms), "ctx"
     )
-    in_sum = lax.psum(in_terms, ("ctx", "chan"))
+    in_sum = jnp.sum(jax.lax.all_gather(in_terms, axis_name=("ctx", "chan")), axis=0)
     return (
         output,
         grad_inputs[0],

time: 659 us -> 645 us (0.979)
  waiting for transfers between devices: 241 us -> 225 us
    all_gather x0 -> x1, blocking collectives: none -> 43.7 us  [body(): jax.lax.all_gather(in_terms, axis_name=('ctx', 'chan'))]
    psum x1 -> x0, blocking collectives: 40.9 us -> none  [body(): in_sum = lax.psum(in_terms, ('ctx', 'chan'))]
    psum x1, waiting for transfers between devices: 21.3 us -> 0.01 us  [body(): lax.psum((short_terms, out_terms, decay_terms, skip_terms), 'ctx')]
    all_to_all x2, waiting for transfers between devices: 7.28 us -> 15.6 us  [to_tokens(): lax.all_to_all(columns, 'ctx', split_axis=0, concat_axis=3, tiled=True)]
  transfers between devices with their start and end apart: 11 -> 11, of which waited for: 10 -> 9; matrix products, arithmetic and copies ran while one was open for 22% -> 23% of each run, Pallas kernels for 0% -> 0%
where the time goes in v1:
time: 645 us; the launch traced here: 637 us
  waiting for transfers between devices  225 us (35%)
  matrix products  161 us (25%)
  local copies, waits for them, and re-layouts  82.8 us (13%)
  blocking collectives  79.4 us (12%)
  starting transfers between devices  44.5 us (7%)
  other arithmetic  28.9 us (4%)
  between operations  15.7 us (2%)
    dot_general x40, matrix products, contract(): return jnp.einsum(form, left, right, precision=PRECISE)  156 us
    all_to_all x2, waiting for transfers between devices, forward_spectrum(): lax.all_to_all(jnp.stack([rows_real, rows_imag]), 'ctx', split_axis=1, co...  97.4 us
    all_to_all x2, waiting for transfers between devices, inverse_columns(): lax.all_to_all(jnp.stack([real_part, imag_part]), 'ctx', split_axis=4, co...  85.6 us
    all_gather x1, blocking collectives, body(): jax.lax.all_gather(in_terms, axis_name=('ctx', 'chan'))  43.7 us
    psum x1, blocking collectives, body(): lax.psum((short_terms, out_terms, decay_terms, skip_terms), 'ctx')  35.7 us
    all_to_all x2, waiting for transfers between devices, forward_spectrum(): lax.all_to_all(signals.reshape((1, signal_count, channels, length)), 'ctx...  26.2 us
    all_to_all x2, waiting for transfers between devices, to_tokens(): lax.all_to_all(columns, 'ctx', split_axis=0, concat_axis=3, tiled=True)  15.6 us
  transfers between devices with their start and end apart: 11, of which 9 were waited for; matrix products, arithmetic and copies ran while one was open for 23% of the time, Pallas kernels for 0%

profile of v1, /device:TPU:0, one launch (start us, length us, event | category | flops | bytes accessed | tf_op | source)
XLA Modules:
  0.0 637.0 jit_solution(16009780104876808809)
XLA Ops:
  11.0 4.8 collective-permute-start
  20.5 6.6 %all-to-all-start.4 = ((f32[1,1,1024,128]{2,1,0,3:T(1,128)}), f32[1,1,1024,128]{2,1,0,3:T(1,128)}, u32[]{:S(2)}, u32[]{:S(2)}) async-start(f32[1,1,1024,128]{2,1,0,3:T(1,128)} %copy.246), calls=%async_computation.4 | async-start | bytes 1048576 | tf_op jit(solution)/shard_map/all_to_all | solution.py:112
  32.8 7.8 %all-to-all-done.4 = f32[1,1,1024,128]{2,1,0,3:T(1,128)} async-done(((f32[1,1,1024,128]{2,1,0,3:T(1,128)}), f32[1,1,1024,128]{2,1,0,3:T(1,128)}, u32[]{:S(2)}, u32[]{:S(2)}) %all-to-all-start.4) | async-done | bytes 524320 | tf_op jit(solution)/shard_map/all_to_all | solution.py:112
  40.6 4.2 all-to-all-start
  51.2 18.4 %all-to-all-done = f32[1,2,1024,128]{2,1,0,3:T(2,128)} async-done(((f32[1,2,1024,128]{2,1,0,3:T(2,128)}), f32[1,2,1024,128]{2,1,0,3:T(2,128)}, u32[]{:S(2)}, u32[]{:S(2)}) %all-to-all-start) | async-done | bytes 1048608 | tf_op jit(solution)/shard_map/all_to_all | solution.py:112
  69.6 4.8 all-to-all-start.5
  74.4 3.4 negate_bitcast_fusion
  77.9 3.4 convolution_bitcast_fusion
  81.9 4.4 copy.220
  86.3 35.7 %all-to-all-done.5 = f32[2,16,1,1024,16]{3,4,2,0,1:T(8,128)} async-done(((f32[2,16,1,1024,16]{3,4,2,0,1:T(8,128)}), f32[2,16,1,1024,16]{3,4,2,0,1:T(8,128)}, u32[]{:S(2)}, u32[]{:S(2)}) %all-to-all-start.5) | async-done | bytes 2097184 | tf_op jit(solution)/shard_map/all_to_all | solution.py:124
  122.0 4.7 all-to-all-start.1
  132.9 4.1 fusion.61
  136.9 4.3 fusion.35
  141.3 4.1 fusion.65
  145.3 5.7 subtract_bitcast_fusion.1
  157.5 61.7 %all-to-all-done.1 = f32[2,16,2,1024,16]{3,4,2,0,1:T(8,128)} async-done(((f32[2,16,2,1024,16]{3,4,2,0,1:T(8,128)}), f32[2,16,2,1024,16]{3,4,2,0,1:T(8,128)}, u32[]{:S(2)}, u32[]{:S(2)}) %all-to-all-start.1) | async-done | bytes 4194336 | tf_op jit(solution)/shard_map/all_to_all | solution.py:124
  224.1 7.9 %fusion.26 = f32[2,2,1024,64,2]{2,4,3,1,0:T(2,128)S(1)} fusion(f32[2,2,1024,2,64]{2,4,3,1,0:T(8,128)S(1)} %get-tuple-element.68), kind=kOutput, calls=%fused_computation.48 | convolution fusion | flops 12582968 | bytes 4194304 | tf_op jit(solution)/shard_map/cb,...ba->...ca/dot_general | solution.py:31
  232.0 8.3 %fusion.22 = f32[2,2,1024,64,2]{2,4,3,1,0:T(2,128)S(1)} fusion(f32[2,2,1024,2,64]{2,4,3,1,0:T(8,128)S(1)} %get-tuple-element.69), kind=kOutput, calls=%fused_computation.44 | convolution fusion | flops 12582968 | bytes 4194304 | tf_op jit(solution)/shard_map/cb,...ba->...ca/dot_general | solution.py:31
  240.3 8.2 %convolution_add_fusion = f32[2,2,1024,64,2]{2,4,3,1,0:T(2,128)S(1)} fusion(f32[2,2,1024,64,2]{2,4,3,1,0:T(2,128)S(1)} %fusion.26, f32[2,2,1024,2,64]{2,4,3,1,0:T(8,128)S(1)} %get-tuple-element.69), kind=kOutput, calls=%fused_computation.42 | convolution fusion | flops 13107256 | bytes 6291456 | tf_op jit(solution)/shard_map/cb,...ba->...ca/dot_general | solution.py:31
  248.6 11.2 %fusion.2 = (f32[2,2,1024,2,64]{2,3,4,1,0:T(2,128)S(1)}, f32[2,2,1024,2,64]{2,3,4,1,0:T(2,128)S(1)}) fusion(f32[2,2,1024,64,2]{2,4,3,1,0:T(2,128)S(1)} %convolution_add_fusion, f32[2,64]{0,1:T(8,128)S(1)} %copy-done.20, f32[2,64]{0,1:T(8,128)S(1)} %copy-done.22, f32[2,2,1024,64,2]{2,4,3,1,0:T(2,128)S(1)} %fusion.22, ...), kind=kOutput, calls=%fused_computation.14 | convolution fusion | flops 16252984 | bytes 10486784 | tf_op jit(solution)/shard_map/cb,...ba->...ca/dot_general | solution.py:31
  265.4 3.1 fusion.16
  268.6 3.1 fusion.19
  271.7 3.9 multiply_subtract_fusion.3
  284.9 9.6 %multiply_subtract_fusion = (f32[2,2,1024,2,64]{2,3,4,1,0:T(2,128)S(1)}, f32[2,2,1024,2,64]{2,3,4,1,0:T(2,128)S(1)}) fusion(f32[2,64]{0,1:T(8,128)S(1)} %copy-done.20, f32[2,64]{0,1:T(8,128)S(1)} %copy-done.22, f32[2,2,1024,2,64]{2,4,3,1,0:T(8,128)S(1)} %fusion.13, f32[2,2,1024,2,64]{2,4,3,1,0:T(8,128)S(1)} %fusion.15, ...), kind=kLoop, calls=%fused_computation.23 | loop fusion | flops 4194304 | bytes 12583936 | tf_op jit(solution)/shard_map/sub | solution.py:39
  294.5 7.5 %fusion.190 = f32[2,2,1024,64,2]{2,4,3,1,0:T(2,128)S(1)} fusion(f32[2,2,1024,2,64]{2,3,4,1,0:T(2,128)S(1)} %get-tuple-element.60), kind=kOutput, calls=%fused_computation.283 | convolution fusion | flops 12582968 | bytes 4194304 | tf_op jit(solution)/shard_map/bc,...ca->...ba/dot_general | solution.py:31
  302.0 7.5 %fusion.188 = f32[2,2,1024,64,2]{2,4,3,1,0:T(2,128)S(1)} fusion(f32[2,2,1024,2,64]{2,3,4,1,0:T(2,128)S(1)} %get-tuple-element.61), kind=kOutput, calls=%fused_computation.281 | convolution fusion | flops 12582968 | bytes 4194304 | tf_op jit(solution)/shard_map/bc,...ca->...ba/dot_general | solution.py:31
  309.6 8.4 %subtract_bitcast_fusion = f32[2,2,1024,2,64]{2,3,4,1,0:T(2,128)S(1)} fusion(f32[2,2,1024,64,2]{2,4,3,1,0:T(2,128)S(1)} %fusion.190, f32[2,2,1024,2,64]{2,3,4,1,0:T(2,128)S(1)} %get-tuple-element.61), kind=kOutput, calls=%fused_computation.21 | convolution fusion | flops 13107256 | bytes 6291456 | tf_op jit(solution)/shard_map/bc,...ca->...ba/dot_general | solution.py:31
  317.9 8.0 %add_bitcast_fusion = f32[2,2,1024,2,64]{2,3,4,1,0:T(2,128)S(1)} fusion(f32[2,2,1024,64,2]{2,4,3,1,0:T(2,128)S(1)} %fusion.188, f32[2,2,1024,2,64]{2,3,4,1,0:T(2,128)S(1)} %get-tuple-element.60), kind=kOutput, calls=%fused_computation.20 | convolution fusion | flops 13107256 | bytes 6291456 | tf_op jit(solution)/shard_map/bc,...ca->...ba/dot_general | solution.py:31
  328.8 5.2 copy.268
  334.0 5.0 all-to-all-start.6
  345.8 4.1 fusion.67
  349.8 4.3 fusion.37
  354.5 4.1 fusion.71
  358.5 4.4 fusion.38
  366.8 64.8 %all-to-all-done.6 = f32[2,2,2,1024,128]{3,2,1,0,4:T(2,128)} async-done(((f32[2,2,2,1024,128]{3,2,1,0,4:T(2,128)}), f32[2,2,2,1024,128]{3,2,1,0,4:T(2,128)}, u32[]{:S(2)}, u32[]{:S(2)}) %all-to-all-start.6) | async-done | bytes 4194336 | tf_op jit(solution)/shard_map/all_to_all | solution.py:149
  431.5 4.4 all-to-all-start.2
  435.9 4.6 copy.269
  445.3 3.7 squeeze.65
  449.1 4.6 copy.270
  453.7 3.7 squeeze.64
  462.9 20.8 %all-to-all-done.2 = f32[2,2,1,1024,128]{3,1,2,0,4:T(2,128)} async-done(((f32[2,2,1,1024,128]{3,1,2,0,4:T(2,128)}), f32[2,2,1,1024,128]{3,1,2,0,4:T(2,128)}, u32[]{:S(2)}, u32[]{:S(2)}) %all-to-all-start.2) | async-done | bytes 2097184 | tf_op jit(solution)/shard_map/all_to_all | solution.py:149
  483.7 4.5 all-to-all-start.7
  496.9 3.0 copy.242
  506.5 7.3 %all-to-all-done.7 = f32[8,2,1024,16]{2,3,1,0:T(8,128)} async-done(((f32[8,2,1024,16]{2,3,1,0:T(8,128)}), f32[8,2,1024,16]{2,3,1,0:T(8,128)}, u32[]{:S(2)}, u32[]{:S(2)}) %all-to-all-start.7) | async-done | bytes 1048608 | tf_op jit(solution)/shard_map/all_to_all | solution.py:162
  513.8 4.1 all-to-all-start.3
  523.7 8.3 %all-to-all-done.3 = f32[8,1,1024,16]{2,3,1,0:T(8,128)} async-done(((f32[8,1,1024,16]{2,3,1,0:T(8,128)}), f32[8,1,1024,16]{2,3,1,0:T(8,128)}, u32[]{:S(2)}, u32[]{:S(2)}) %all-to-all-start.3) | async-done | bytes 524320 | tf_op jit(solution)/shard_map/all_to_all | solution.py:162
  539.1 35.7 %all-reduce = (f32[3,3,1024]{2,0,1:T(4,128)S(1)}, f32[1024]{0:T(1024)S(1)}, f32[1024]{0:T(1024)S(1)}) all-reduce(f32[3,3,1024]{2,0,1:T(4,128)S(1)} %pad_maximum_fusion.14, f32[1024]{0:T(1024)S(1)} %get-tuple-element.106, f32[1024]{0:T(1024)S(1)} %get-tuple-element.96), channel_id=1, replica_groups=mesh['ctx'=8,'chan'=4] {'ctx'}, use_global_device_ids=true, to_apply=%region_3.4 | all-reduce | flops 11264 | bytes 90112 | tf_op jit(solution)/shard_map/psum | solution.py:244
  577.3 43.7 %all-gather = f32[2048,64]{1,0:T(8,128)S(1)} all-gather(f32[64,64]{1,0:T(8,128)S(1)} %copy-done.23), channel_id=2, replica_groups=mesh['ctx'=8,'chan'=4] {'ctx','chan'}, dimensions={0}, use_global_device_ids=true | all-gather | bytes 540672 | tf_op jit(solution)/shard_map/all_gather | solution.py:247
  (189 shorter events, 116.4 us)
Async XLA Ops:
  7.2 22.2 %copy-start = (f32[64,1024]{1,0:T(8,128)S(1)}, f32[64,1024]{1,0:T(8,128)}, u32[]{:S(2)}) copy-start(f32[64,1024]{1,0:T(8,128)} %param.14) | copy-start | bytes 786436
  8.3 2.6 copy-start.9
  8.3 7.5 %copy-start.27 = (f32[3,3,1024]{2,1,0:T(4,128)S(1)}, f32[3,3,1024]{2,1,0:T(4,128)}, u32[]{:S(2)}) copy-start(f32[3,3,1024]{2,1,0:T(4,128)} %param.12) | copy-start | bytes 110596
  8.3 7.7 %copy-start.36 = (f32[1024]{0:T(1024)S(1)}, f32[1024]{0:T(1024)}, u32[]{:S(2)}) copy-start(f32[1024]{0:T(1024)} %param.15) | copy-start | bytes 12292
  8.4 7.8 %copy-start.18 = (bf16[1024,128]{1,0:T(8,128)(2,1)S(1)}, bf16[1024,128]{1,0:T(8,128)(2,1)}, u32[]{:S(2)}) copy-start(bf16[1024,128]{1,0:T(8,128)(2,1)} %param.17) | copy-start | bytes 786436
  9.6 7.4 %copy-start.10 = (bf16[1024,128]{0,1:T(8,128)(2,1)}, bf16[1024,128]{0,1:T(8,128)(2,1)S(1)}, u32[]{:S(2)}) copy-start(bf16[1024,128]{0,1:T(8,128)(2,1)S(1)} %copy.215) | copy-start | bytes 786436
  10.8 6.5 %copy-start.11 = (bf16[1024,128]{0,1:T(8,128)(2,1)}, bf16[1024,128]{0,1:T(8,128)(2,1)S(1)}, u32[]{:S(2)}) copy-start(bf16[1024,128]{0,1:T(8,128)(2,1)S(1)} %copy.216) | copy-start | bytes 786436
  11.0 6.2 collective-permute-start
  17.3 1.8 copy-start.25
  17.3 1.7 copy-start.17
  20.5 20.0 %all-to-all-start.4 = ((f32[1,1,1024,128]{2,1,0,3:T(1,128)}), f32[1,1,1024,128]{2,1,0,3:T(1,128)}, u32[]{:S(2)}, u32[]{:S(2)}) async-start(f32[1,1,1024,128]{2,1,0,3:T(1,128)} %copy.246), calls=%async_computation.4 | async-start | bytes 1048576 | tf_op jit(solution)/shard_map/all_to_all | solution.py:112
  27.7 1.7 copy-start.37
  30.1 0.8 copy-start.7
  40.6 29.0 %all-to-all-start = ((f32[1,2,1024,128]{2,1,0,3:T(2,128)}), f32[1,2,1024,128]{2,1,0,3:T(2,128)}, u32[]{:S(2)}, u32[]{:S(2)}) async-start(f32[1,2,1024,128]{2,1,0,3:T(2,128)} %copy.217), calls=%async_computation | async-start | bytes 2097152 | tf_op jit(solution)/shard_map/all_to_all | solution.py:112
  69.6 52.4 %all-to-all-start.5 = ((f32[2,16,1,1024,16]{3,4,2,0,1:T(8,128)}), f32[2,16,1,1024,16]{3,4,2,0,1:T(8,128)}, u32[]{:S(2)}, u32[]{:S(2)}) async-start(f32[2,16,1,1024,16]{3,4,2,0,1:T(8,128)} %copy.248), calls=%async_computation.5 | async-start | bytes 4194304 | tf_op jit(solution)/shard_map/all_to_all | solution.py:124
  122.0 97.3 %all-to-all-start.1 = ((f32[2,16,2,1024,16]{3,4,2,0,1:T(8,128)}), f32[2,16,2,1024,16]{3,4,2,0,1:T(8,128)}, u32[]{:S(2)}, u32[]{:S(2)}) async-start(f32[2,16,2,1024,16]{3,4,2,0,1:T(8,128)} %copy.220), calls=%async_computation.1 | async-start | bytes 8388608 | tf_op jit(solution)/shard_map/all_to_all | solution.py:124
  127.4 2.1 copy-start.30
  130.3 2.2 copy-start.28
  141.2 4.1 copy-start.19
  141.2 4.1 copy-start.21
  151.1 4.0 copy-start.14
  222.6 0.7 copy-start.29
  240.3 8.3 %copy-start.20 = (f32[2,64]{0,1:T(8,128)S(1)}, f32[2,64]{0,1:T(8,128)}, u32[]{:S(2)}) copy-start(f32[2,64]{0,1:T(8,128)} %copy.229) | copy-start | bytes 1540
  240.3 8.3 %copy-start.22 = (f32[2,64]{0,1:T(8,128)S(1)}, f32[2,64]{0,1:T(8,128)}, u32[]{:S(2)}) copy-start(f32[2,64]{0,1:T(8,128)} %copy.226) | copy-start | bytes 1540
  268.5 3.1 copy-start.13
  268.6 3.1 copy-start.15
  268.6 3.1 copy-start.16
  326.5 0.7 copy-start.33
  334.0 97.5 %all-to-all-start.6 = ((f32[2,2,2,1024,128]{3,2,1,0,4:T(2,128)}), f32[2,2,2,1024,128]{3,2,1,0,4:T(2,128)}, u32[]{:S(2)}, u32[]{:S(2)}) async-start(f32[2,2,2,1024,128]{3,2,1,0,4:T(2,128)} %copy.268), calls=%async_computation.6 | async-start | bytes 8388608 | tf_op jit(solution)/shard_map/all_to_all | solution.py:149
  339.0 2.6 copy-start.1
  339.0 3.8 copy-start.2
  342.9 1.3 copy-start.31
  342.9 1.3 copy-start.32
  358.5 4.7 copy-start.35
  431.5 52.2 %all-to-all-start.2 = ((f32[2,2,1,1024,128]{3,1,2,0,4:T(2,128)}), f32[2,2,1,1024,128]{3,1,2,0,4:T(2,128)}, u32[]{:S(2)}, u32[]{:S(2)}) async-start(f32[2,2,1,1024,128]{3,1,2,0,4:T(2,128)} %copy.240), calls=%async_computation.2 | async-start | bytes 4194304 | tf_op jit(solution)/shard_map/all_to_all | solution.py:149
  457.3 2.9 copy-start.3
  483.7 30.1 %all-to-all-start.7 = ((f32[8,2,1024,16]{2,3,1,0:T(8,128)}), f32[8,2,1024,16]{2,3,1,0:T(8,128)}, u32[]{:S(2)}, u32[]{:S(2)}) async-start(f32[8,2,1024,16]{2,3,1,0:T(8,128)} %copy.272), calls=%async_computation.7 | async-start | bytes 2097152 | tf_op jit(solution)/shard_map/all_to_all | solution.py:162
  502.8 2.0 copy-start.12
  513.8 18.2 %all-to-all-start.3 = ((f32[8,1,1024,16]{2,3,1,0:T(8,128)}), f32[8,1,1024,16]{2,3,1,0:T(8,128)}, u32[]{:S(2)}, u32[]{:S(2)}) async-start(f32[8,1,1024,16]{2,3,1,0:T(8,128)} %copy.244), calls=%async_computation.3 | async-start | bytes 1048576 | tf_op jit(solution)/shard_map/all_to_all | solution.py:162
  517.9 110.2 %all-reduce.3.cloned.1.call-start = ((), (), s32[]{:S(2)}) async-start(), calls=%async_computation.8 | async-start | bytes 524288 | tf_op jit(solution)/shard_map/psum | solution.py:244
  518.0 2.2 copy-start.8
  518.0 3.1 copy-start.24
  532.0 4.7 copy-start.26
  536.7 40.6 %copy-start.23 = (f32[64,64]{1,0:T(8,128)S(1)}, f32[64,64]{1,0:T(8,128)}, u32[]{:S(2)}) copy-start(f32[64,64]{1,0:T(8,128)} %fusion.105) | copy-start | bytes 49156
  576.0 47.4 %collective-permute-start.1 = (f32[3,1024,2]{1,2,0:T(2,128)}, f32[3,1024,2]{1,2,0:T(2,128)}, u32[]{:S(2)}, u32[]{:S(2)}) collective-permute-start(f32[3,1024,2]{1,2,0:T(2,128)} %slice.161), channel_id=1, source_target_pairs={{4,0},{8,4},{12,8},{16,12},{20,16},{24,20},{28,24},{5,1},{9,5},{13... | collective-permute-start | bytes 73736 | tf_op jit(solution)/shard_map/ppermute | solution.py:13
  622.5 1.7 copy-start.4
  622.5 1.7 copy-start.5
  622.5 1.7 copy-start.6
  (1 other events, 0.7 us)
Sparse Core Ops, SparseCore 0:
  536.8 70.1 all-reduce.2
